TPU v7x, 32 devices: a whole 2x2x4 slice. The times are simulated.
32 devices in a mesh: frame: 4 (over x, core), within: 8 (over z, y).
Axes of the slice: x: 2, y: 2, z: 4, core: 2. Of those that a mesh axis runs over, the one named last changes fastest.
Arguments:
- queries: bfloat16 [4, 576, 1024], P('frame', 'within'), may hold values from -6 to 6
- keys_in: bfloat16 [4, 576, 1024], P('frame', 'within'), may hold values from -6 to 6
- values_in: bfloat16 [4, 576, 1024], P('frame', 'within'), may hold values from -6 to 6
- grad_out: bfloat16 [4, 576, 1024], P('frame', 'within'), may hold values from -6 to 6
- partners: int32 [4, 2], replicated, may hold values from 0 to 3
- registers: int32 [4], replicated, may hold values from 1 to 144
Outputs:
- grad_queries: bfloat16 [4, 576, 1024], P('frame', 'within')
- grad_keys: bfloat16 [4, 576, 1024], P('frame', 'within')
- grad_values: bfloat16 [4, 576, 1024], P('frame', 'within')
Inputs may be any that keep to these rules, and one draw needn't show every extreme that they name: `partners`: A row may list a group more than once, and may list its own group.
All inputs are finite; a program needn't handle non-finite values.
Results may differ from a plain program's by a relative error of at most 0.012.
Values may be sent and summed in bfloat16 or wider, within the bound.
A program may use at most 128 MiB of HBM per device.

v0:
```python
import jax
import jax.numpy as jnp
from jax import lax
from jax.sharding import PartitionSpec as P

DH = 64


def local(queries, keys_in, values_in, grad_out, partners, registers):
    q_wide, k_wide, v_wide, d_wide = (
        lax.all_to_all(queries, "within", split_axis=2, concat_axis=1, tiled=True),
        lax.all_to_all(keys_in, "within", split_axis=2, concat_axis=1, tiled=True),
        lax.all_to_all(values_in, "within", split_axis=2, concat_axis=1, tiled=True),
        lax.all_to_all(grad_out, "within", split_axis=2, concat_axis=1, tiled=True),
    )
    seq = q_wide.shape[1]
    cols = q_wide.shape[2]
    heads_here = cols // DH
    scale = DH ** (-0.5)

    def split_heads(block):
        return block.reshape(seq, heads_here, DH)

    query3 = split_heads(q_wide[0])
    key3 = split_heads(k_wide[0])
    value3 = split_heads(v_wide[0])
    cotan3 = split_heads(d_wide[0])
    group = lax.axis_index("frame")
    listed = partners[group]
    positions = jnp.arange(seq, dtype=jnp.int32)
    everyone = jnp.ones((seq,), jnp.float32)
    groups = lax.axis_size("frame") * queries.shape[0]

    def patches(other):
        return (positions >= registers[other]).astype(jnp.float32)

    def logits(keys_here, visible):
        raw = (
            jnp.einsum("qhd,khd->hqk", query3, keys_here, preferred_element_type=jnp.float32)
            * scale
        )
        return jnp.where(visible[None, None, :] > 0, raw, -1e30)

    def stats(state, keys_here, values_here, visible, weight):
        old_top, old_total, old_dsum = state
        raw = logits(keys_here, visible)
        top = jnp.max(raw, axis=2)
        expo = jnp.exp(raw - top[:, :, None])
        dprod = jnp.einsum("qhd,khd->hqk", cotan3, values_here, preferred_element_type=jnp.float32)
        total = weight * jnp.sum(expo, axis=2)
        dsum = weight * jnp.sum(expo * dprod, axis=2)
        new_top = jnp.maximum(old_top, top)
        keep_old = jnp.exp(old_top - new_top)
        keep_new = jnp.exp(top - new_top)
        return (
            new_top,
            old_total * keep_old + total * keep_new,
            old_dsum * keep_old + dsum * keep_new,
        )

    def grads(final, keys_here, values_here, visible, weight):
        top, total, delta = final
        raw = logits(keys_here, visible)
        prob = jnp.exp(raw - top[:, :, None]) / total[:, :, None]
        dprod = jnp.einsum("qhd,khd->hqk", cotan3, values_here, preferred_element_type=jnp.float32)
        dscore = prob * (dprod - delta[:, :, None])
        dscore_low = dscore.astype(jnp.bfloat16)
        dq_add = jnp.einsum(
            "hqk,khd->qhd", dscore_low, keys_here, preferred_element_type=jnp.float32
        ) * (scale * weight)
        prob_low = prob.astype(jnp.bfloat16)
        dk_add = jnp.einsum(
            "hqk,qhd->khd", dscore_low, query3, preferred_element_type=jnp.float32
        ) * (scale * weight)
        dv_add = (
            jnp.einsum("hqk,qhd->khd", prob_low, cotan3, preferred_element_type=jnp.float32)
            * weight
        )
        return (dq_add.reshape(seq, cols), dk_add.reshape(seq, cols), dv_add.reshape(seq, cols))

    blank = jnp.zeros((heads_here, seq), jnp.float32)
    state = stats((blank - 1e30, blank, blank), key3, value3, everyone, 1.0)
    keys_all, values_all = (
        lax.all_gather(k_wide, "frame", axis=0, tiled=True),
        lax.all_gather(v_wide, "frame", axis=0, tiled=True),
    )
    for slot in range(listed.shape[0]):
        other = listed[slot]
        state = stats(
            state, split_heads(keys_all[other]), split_heads(values_all[other]), patches(other), 1.0
        )
    top, total, dsum = state
    final = (top, total, dsum / total)
    own_terms = grads(final, key3, value3, everyone, 1.0)
    empty = jnp.zeros((groups, seq, cols), jnp.float32)
    results = (own_terms[0], empty.at[group].add(own_terms[1]), empty.at[group].add(own_terms[2]))
    for slot in range(listed.shape[0]):
        other = listed[slot]
        added = grads(
            final, split_heads(keys_all[other]), split_heads(values_all[other]), patches(other), 1.0
        )
        results = (
            results[0] + added[0],
            results[1].at[other].add(added[1]),
            results[2].at[other].add(added[2]),
        )
    dq_sum = results[0]
    got_keys, got_values = (
        lax.all_to_all(results[1], "frame", split_axis=0, concat_axis=0, tiled=True),
        lax.all_to_all(results[2], "frame", split_axis=0, concat_axis=0, tiled=True),
    )
    dk_mine = jnp.sum(got_keys, axis=0, keepdims=True)
    dv_mine = jnp.sum(got_values, axis=0, keepdims=True)
    dq_low = dq_sum.astype(jnp.bfloat16)[None]
    dk_low = dk_mine.astype(jnp.bfloat16)
    dv_low = dv_mine.astype(jnp.bfloat16)
    return (
        lax.all_to_all(dq_low, "within", split_axis=1, concat_axis=2, tiled=True),
        lax.all_to_all(dk_low, "within", split_axis=1, concat_axis=2, tiled=True),
        lax.all_to_all(dv_low, "within", split_axis=1, concat_axis=2, tiled=True),
    )


def solution(mesh):
    placed = (
        P("frame", "within", None),
        P("frame", "within", None),
        P("frame", "within", None),
        P("frame", "within", None),
        P(),
        P(),
    )
    return jax.shard_map(
        local,
        mesh=mesh,
        in_specs=placed,
        out_specs=(
            P("frame", "within", None),
            P("frame", "within", None),
            P("frame", "within", None),
        ),
        check_vma=False,
    )
```

profile of v0, /device:TPU:0, one launch (start us, length us, event | category | flops | bytes accessed | tf_op | source)
XLA Modules:
  0.0 192.7 jit_solution(5798555888546599513)
XLA Ops:
  6.1 7.3 %all-to-all-start.1 = ((bf16[8,2,4608]{2,1,0:T(2,128)(2,1)}), bf16[8,2,4608]{2,1,0:T(2,128)(2,1)S(1)}, u32[]{:S(2)}, u32[]{:S(2)}) async-start(bf16[8,2,4608]{2,1,0:T(2,128)(2,1)} %reshape.379), calls=%async_computation.1 | async-start | bytes 294912 | tf_op jit(solution)/shard_map/all_to_all | solution.py:12
  18.0 2.4 %reduce.30 = bf16[1024,72]{1,0:T(8,128)(2,1)S(1)} reduce(bf16[1024,1,72]{2,1,0:T(2,128)(2,1)S(1)} %bitcast.221, bf16[]{:T(256)} %broadcast.248), dimensions={1}, to_apply=%bitcast.170.reduce_sub_computation | reduce | bytes 294914
  24.3 6.0 %all-to-all-start.3 = ((bf16[8,2,4608]{2,1,0:T(2,128)(2,1)}), bf16[8,2,4608]{2,1,0:T(2,128)(2,1)S(1)}, u32[]{:S(2)}, u32[]{:S(2)}) async-start(bf16[8,2,4608]{2,1,0:T(2,128)(2,1)} %reshape.381), calls=%async_computation.3 | async-start | bytes 294912 | tf_op jit(solution)/shard_map/all_to_all | solution.py:13
  40.9 6.0 %all-to-all-start = ((bf16[8,2,4608]{2,1,0:T(2,128)(2,1)}), bf16[8,2,4608]{2,1,0:T(2,128)(2,1)S(1)}, u32[]{:S(2)}, u32[]{:S(2)}) async-start(bf16[8,2,4608]{2,1,0:T(2,128)(2,1)} %reshape.385), calls=%async_computation | async-start | bytes 294912 | tf_op jit(solution)/shard_map/all_to_all | solution.py:11
  48.2 7.5 %all_gather.6 = bf16[4,576,128]{2,1,0:T(8,128)(2,1)S(1)} all-gather(bf16[1,576,128]{2,1,0:T(8,128)(2,1)S(1)} %bitcast.249), channel_id=1, replica_groups=mesh['frame'=4,'within'=8] {'frame'}, dimensions={0}, use_global_device_ids=true | all-gather | bytes 737280 | tf_op jit(solution)/shard_map/all_gather | solution.py:84
  55.8 7.6 %all_gather.7 = bf16[4,576,128]{2,1,0:T(8,128)(2,1)S(1)} all-gather(bf16[1,576,128]{2,1,0:T(8,128)(2,1)S(1)} %bitcast.254), channel_id=1, replica_groups=mesh['frame'=4,'within'=8] {'frame'}, dimensions={0}, use_global_device_ids=true | all-gather | bytes 737280 | tf_op jit(solution)/shard_map/all_gather | solution.py:85
  63.4 6.0 %all-to-all-start.2 = ((bf16[8,2,4608]{2,1,0:T(2,128)(2,1)}), bf16[8,2,4608]{2,1,0:T(2,128)(2,1)S(1)}, u32[]{:S(2)}, u32[]{:S(2)}) async-start(bf16[8,2,4608]{2,1,0:T(2,128)(2,1)} %reshape.383), calls=%async_computation.2 | async-start | bytes 294912 | tf_op jit(solution)/shard_map/all_to_all | solution.py:14
  73.3 3.9 %all-to-all-done.2 = bf16[8,2,4608]{2,1,0:T(2,128)(2,1)S(1)} async-done(((bf16[8,2,4608]{2,1,0:T(2,128)(2,1)}), bf16[8,2,4608]{2,1,0:T(2,128)(2,1)S(1)}, u32[]{:S(2)}, u32[]{:S(2)}) %all-to-all-start.2) | async-done | bytes 147488 | tf_op jit(solution)/shard_map/all_to_all | solution.py:14
  85.5 2.8 %fusion.14 = (f32[2,576]{1,0:T(2,128)S(1)}, f32[2,576]{1,0:T(2,128)S(1)}, f32[2,576,576]{2,1,0:T(8,128)}) fusion(f32[2,576,576]{2,1,0:T(8,128)S(1)} %get-tuple-element.99, f32[2,576]{1,0:T(2,128)S(1)} %get-tuple-element.98, pred[576]{0:T(1024)(128)(4,1)S(1)} %get-tuple-element.109, bf16[576,2,64]{0,2,1:T(8,128)(2,1)S(1)} %bitcast.238, ...), kind=kOutput, calls=%fused_computation.30 | convolution fusion | flops 88913664 | bytes 5617728 | tf_op jit(solution)/shard_map/qhd,khd->hqk/dot_general | solution.py:49
  88.3 2.8 %fusion.13 = (f32[2,576]{1,0:T(2,128)S(1)}, f32[2,576]{1,0:T(2,128)S(1)}, f32[2,576,576]{2,1,0:T(8,128)}) fusion(f32[2,576,576]{2,1,0:T(8,128)S(1)} %get-tuple-element.102, f32[2,576]{1,0:T(2,128)S(1)} %get-tuple-element.101, pred[576]{0:T(1024)(128)(4,1)S(1)} %get-tuple-element.110, bf16[576,2,64]{0,2,1:T(8,128)(2,1)S(1)} %bitcast.239, ...), kind=kOutput, calls=%fused_computation.29 | convolution fusion | flops 88913664 | bytes 5617728 | tf_op jit(solution)/shard_map/qhd,khd->hqk/dot_general | solution.py:49
  91.0 2.5 %fusion.12 = (f32[2,576]{1,0:T(2,128)S(1)}, f32[2,576]{1,0:T(2,128)S(1)}, f32[2,576,576]{1,2,0:T(8,128)}) fusion(f32[2,576,576]{1,2,0:T(8,128)S(1)} %get-tuple-element.105, f32[2,576]{1,0:T(2,128)S(1)} %get-tuple-element.104, bf16[576,2,64]{0,2,1:T(8,128)(2,1)S(1)} %reshape_squeeze.32, bf16[576,2,64]{0,2,1:T(8,128)(2,1)S(1)} %copy-done.14), kind=kOutput, calls=%fused_computation.28 | convolution fusion | flops 88250112 | bytes 5617152 | tf_op jit(solution)/shard_map/qhd,khd->hqk/dot_general | solution.py:65
  104.5 7.0 %fusion.5 = (bf16[2,576,576]{1,2,0:T(8,128)(2,1)S(1)}, bf16[2,576,576]{1,2,0:T(8,128)(2,1)S(1)}, bf16[2,576,576]{1,2,0:T(8,128)(2,1)S(1)}) fusion(f32[2,576,576]{2,1,0:T(8,128)} %get-tuple-element.103, f32[2,576]{1,0:T(2,128)S(1)} %get-tuple-element.88, f32[2,576]{1,0:T(2,128)S(1)} %get-tuple-element.87, f32[2,576]{1,0:T(2,128)S(1)} %get-tuple-element.92, ...), kind=kLoop, calls=%fused_computation.9 | loop fusion | flops 13271040 | bytes 19921536 | tf_op jit(solution)/shard_map/convert_element_type | solution.py:67
  116.1 4.0 %all-to-all-start.4 = ((bf16[8,2,4608]{2,1,0:T(2,128)(2,1)}), bf16[8,2,4608]{2,1,0:T(2,128)(2,1)}, u32[]{:S(2)}, u32[]{:S(2)}) async-start(bf16[8,2,4608]{2,1,0:T(2,128)(2,1)} %reshape.387), calls=%async_computation.4 | async-start | bytes 294912 | tf_op jit(solution)/shard_map/all_to_all | solution.py:118
  121.9 2.5 %fusion.33 = f32[4,576,128]{2,1,0:T(8,128)} fusion(f32[4,576,128]{2,1,0:T(8,128)} %constant_dynamic-update-slice_fusion, s32[]{:T(128)} %select_n.49, f32[1,576,128]{2,1,0:T(8,128)} %copy.143, pred[]{:T(512)} %get-tuple-element.82), kind=kLoop, calls=%fused_computation.58 | loop fusion | flops 147456 | bytes 885760 | tf_op jit(solution)/shard_map/scatter-add | solution.py:105
  124.5 2.4 %fusion.34 = f32[4,576,128]{2,1,0:T(8,128)} fusion(f32[4,576,128]{2,1,0:T(8,128)} %fusion.33, s32[]{:T(128)} %select_n.52, f32[1,576,128]{2,1,0:T(8,128)S(1)} %copy-done.12, pred[]{:T(512)} %get-tuple-element.81), kind=kLoop, calls=%fused_computation.59 | loop fusion | flops 147456 | bytes 885760 | tf_op jit(solution)/shard_map/scatter-add | solution.py:105
  128.0 4.4 %all-to-all-start.7 = ((f32[4,576,128]{2,1,0:T(8,128)}), f32[4,576,128]{2,1,0:T(8,128)}, u32[]{:S(2)}, u32[]{:S(2)}) async-start(f32[4,576,128]{2,1,0:T(8,128)} %fusion.34), calls=%async_computation.7 | async-start | bytes 2359296 | tf_op jit(solution)/shard_map/all_to_all | solution.py:110
  139.9 2.4 %fusion.32 = f32[4,576,128]{2,1,0:T(8,128)} fusion(f32[4,576,128]{2,1,0:T(8,128)} %fusion.31, s32[]{:T(128)} %select_n.52, f32[1,576,128]{2,1,0:T(8,128)S(1)} %copy.136, pred[]{:T(512)} %get-tuple-element.81), kind=kLoop, calls=%fused_computation.57 | loop fusion | flops 147456 | bytes 885760 | tf_op jit(solution)/shard_map/scatter-add | solution.py:104
  142.3 6.1 %all-to-all-done.7 = f32[4,576,128]{2,1,0:T(8,128)} async-done(((f32[4,576,128]{2,1,0:T(8,128)}), f32[4,576,128]{2,1,0:T(8,128)}, u32[]{:S(2)}, u32[]{:S(2)}) %all-to-all-start.7) | async-done | bytes 1179680 | tf_op jit(solution)/shard_map/all_to_all | solution.py:110
  148.3 3.5 %all-to-all-start.5 = ((f32[4,576,128]{2,1,0:T(8,128)}), f32[4,576,128]{2,1,0:T(8,128)S(1)}, u32[]{:S(2)}, u32[]{:S(2)}) async-start(f32[4,576,128]{2,1,0:T(8,128)} %fusion.32), calls=%async_computation.5 | async-start | bytes 2359296 | tf_op jit(solution)/shard_map/all_to_all | solution.py:109
  155.8 11.9 %all-to-all-done.5 = f32[4,576,128]{2,1,0:T(8,128)S(1)} async-done(((f32[4,576,128]{2,1,0:T(8,128)}), f32[4,576,128]{2,1,0:T(8,128)S(1)}, u32[]{:S(2)}, u32[]{:S(2)}) %all-to-all-start.5) | async-done | bytes 1179680 | tf_op jit(solution)/shard_map/all_to_all | solution.py:109
  167.7 5.9 %all-to-all-start.8 = ((bf16[8,2,4608]{2,1,0:T(2,128)(2,1)}), bf16[8,2,4608]{2,1,0:T(2,128)(2,1)S(1)}, u32[]{:S(2)}, u32[]{:S(2)}) async-start(bf16[8,2,4608]{2,1,0:T(2,128)(2,1)} %reshape.391), calls=%async_computation.8 | async-start | bytes 294912 | tf_op jit(solution)/shard_map/all_to_all | solution.py:120
  176.3 4.8 %all-to-all-done.8 = bf16[8,2,4608]{2,1,0:T(2,128)(2,1)S(1)} async-done(((bf16[8,2,4608]{2,1,0:T(2,128)(2,1)}), bf16[8,2,4608]{2,1,0:T(2,128)(2,1)S(1)}, u32[]{:S(2)}, u32[]{:S(2)}) %all-to-all-start.8) | async-done | bytes 147488 | tf_op jit(solution)/shard_map/all_to_all | solution.py:120
  181.0 3.4 %all-to-all-start.6 = ((bf16[8,2,4608]{2,1,0:T(2,128)(2,1)}), bf16[8,2,4608]{2,1,0:T(2,128)(2,1)S(1)}, u32[]{:S(2)}, u32[]{:S(2)}) async-start(bf16[8,2,4608]{2,1,0:T(2,128)(2,1)} %reshape.389), calls=%async_computation.6 | async-start | bytes 294912 | tf_op jit(solution)/shard_map/all_to_all | solution.py:119
  187.4 4.4 %all-to-all-done.6 = bf16[8,2,4608]{2,1,0:T(2,128)(2,1)S(1)} async-done(((bf16[8,2,4608]{2,1,0:T(2,128)(2,1)}), bf16[8,2,4608]{2,1,0:T(2,128)(2,1)S(1)}, u32[]{:S(2)}, u32[]{:S(2)}) %all-to-all-start.6) | async-done | bytes 147488 | tf_op jit(solution)/shard_map/all_to_all | solution.py:119
  (138 shorter events, 70.0 us)
Async XLA Ops:
  0.6 12.7 %copy-start = (s32[4,2]{0,1:T(2,128)S(1)}, s32[4,2]{0,1:T(2,128)}, u32[]{:S(2)}) copy-start(s32[4,2]{0,1:T(2,128)} %param.22) | copy-start | bytes 100
  0.6 22.9 %copy-start.19 = (s32[3]{0:T(128)S(1)}, s32[3]{0:T(128)}, u32[]{:S(2)}) copy-start(s32[3]{0:T(128)} %constant.142.clone.1) | copy-start | bytes 40
  0.7 22.2 %copy-start.18 = (s32[4]{0:T(128)S(1)}, s32[4]{0:T(128)}, u32[]{:S(2)}) copy-start(s32[4]{0:T(128)} %param.23) | copy-start | bytes 52
  0.7 31.0 %copy-start.16 = (bf16[1,72,1024]{2,1,0:T(8,128)(2,1)S(1)}, bf16[1,72,1024]{2,1,0:T(8,128)(2,1)}, u32[]{:S(2)}) copy-start(bf16[1,72,1024]{2,1,0:T(8,128)(2,1)} %param.18) | copy-start | bytes 442372
  2.0 33.7 %copy-start.17 = (bf16[1,72,1024]{2,1,0:T(8,128)(2,1)S(1)}, bf16[1,72,1024]{2,1,0:T(8,128)(2,1)}, u32[]{:S(2)}) copy-start(bf16[1,72,1024]{2,1,0:T(8,128)(2,1)} %param.21) | copy-start | bytes 442372
  6.1 18.3 %all-to-all-start.1 = ((bf16[8,2,4608]{2,1,0:T(2,128)(2,1)}), bf16[8,2,4608]{2,1,0:T(2,128)(2,1)S(1)}, u32[]{:S(2)}, u32[]{:S(2)}) async-start(bf16[8,2,4608]{2,1,0:T(2,128)(2,1)} %reshape.379), calls=%async_computation.1 | async-start | bytes 294912 | tf_op jit(solution)/shard_map/all_to_all | solution.py:12
  24.3 16.6 %all-to-all-start.3 = ((bf16[8,2,4608]{2,1,0:T(2,128)(2,1)}), bf16[8,2,4608]{2,1,0:T(2,128)(2,1)S(1)}, u32[]{:S(2)}, u32[]{:S(2)}) async-start(bf16[8,2,4608]{2,1,0:T(2,128)(2,1)} %reshape.381), calls=%async_computation.3 | async-start | bytes 294912 | tf_op jit(solution)/shard_map/all_to_all | solution.py:13
  40.9 22.5 %all-to-all-start = ((bf16[8,2,4608]{2,1,0:T(2,128)(2,1)}), bf16[8,2,4608]{2,1,0:T(2,128)(2,1)S(1)}, u32[]{:S(2)}, u32[]{:S(2)}) async-start(bf16[8,2,4608]{2,1,0:T(2,128)(2,1)} %reshape.385), calls=%async_computation | async-start | bytes 294912 | tf_op jit(solution)/shard_map/all_to_all | solution.py:11
  63.4 13.7 %all-to-all-start.2 = ((bf16[8,2,4608]{2,1,0:T(2,128)(2,1)}), bf16[8,2,4608]{2,1,0:T(2,128)(2,1)S(1)}, u32[]{:S(2)}, u32[]{:S(2)}) async-start(bf16[8,2,4608]{2,1,0:T(2,128)(2,1)} %reshape.383), calls=%async_computation.2 | async-start | bytes 294912 | tf_op jit(solution)/shard_map/all_to_all | solution.py:14
  84.8 8.8 %copy-start.1 = (f32[2,576,576]{2,1,0:T(8,128)}, f32[2,576,576]{2,1,0:T(8,128)S(1)}, u32[]{:S(2)}) copy-start(f32[2,576,576]{2,1,0:T(8,128)S(1)} %get-tuple-element.99) | copy-start | bytes 7962628
  85.5 9.8 %copy-start.2 = (f32[2,576,576]{2,1,0:T(8,128)}, f32[2,576,576]{2,1,0:T(8,128)S(1)}, u32[]{:S(2)}) copy-start(f32[2,576,576]{2,1,0:T(8,128)S(1)} %get-tuple-element.102) | copy-start | bytes 7962628
  85.5 2.8 %copy-start.15 = (bf16[1,576,128]{1,2,0:T(8,128)(2,1)S(1)}, bf16[1,576,128]{1,2,0:T(8,128)(2,1)}, u32[]{:S(2)}) copy-start(bf16[1,576,128]{1,2,0:T(8,128)(2,1)} %copy.124) | copy-start | bytes 442372
  104.5 7.0 %copy-start.10 = (bf16[576,2,64]{0,2,1:T(8,128)(2,1)S(1)}, bf16[576,2,64]{0,2,1:T(8,128)(2,1)}, u32[]{:S(2)}) copy-start(bf16[576,2,64]{0,2,1:T(8,128)(2,1)} %reshape_squeeze.29) | copy-start | bytes 442372
  104.5 7.4 %copy-start.9 = (bf16[1,576,128]{1,2,0:T(8,128)(2,1)S(1)}, bf16[1,576,128]{1,2,0:T(8,128)(2,1)}, u32[]{:S(2)}) copy-start(bf16[1,576,128]{1,2,0:T(8,128)(2,1)} %copy.116) | copy-start | bytes 442372
  112.4 8.8 %copy-start.11 = (f32[1,576,128]{2,1,0:T(8,128)S(1)}, f32[1,576,128]{2,1,0:T(8,128)}, u32[]{:S(2)}) copy-start(f32[1,576,128]{2,1,0:T(8,128)} %copy.141) | copy-start | bytes 884740
  113.5 10.9 %copy-start.12 = (f32[1,576,128]{2,1,0:T(8,128)S(1)}, f32[1,576,128]{2,1,0:T(8,128)}, u32[]{:S(2)}) copy-start(f32[1,576,128]{2,1,0:T(8,128)} %copy.145) | copy-start | bytes 884740
  113.5 13.3 %copy-start.8 = (bf16[2,576,576]{1,2,0:T(8,128)(2,1)S(1)}, bf16[2,576,576]{1,2,0:T(8,128)(2,1)}, u32[]{:S(2)}) copy-start(bf16[2,576,576]{1,2,0:T(8,128)(2,1)} %copy-done.7) | copy-start | bytes 3981316
  116.1 11.9 %all-to-all-start.4 = ((bf16[8,2,4608]{2,1,0:T(2,128)(2,1)}), bf16[8,2,4608]{2,1,0:T(2,128)(2,1)}, u32[]{:S(2)}, u32[]{:S(2)}) async-start(bf16[8,2,4608]{2,1,0:T(2,128)(2,1)} %reshape.387), calls=%async_computation.4 | async-start | bytes 294912 | tf_op jit(solution)/shard_map/all_to_all | solution.py:118
  121.9 10.5 %copy-start.4 = (bf16[2,576,576]{1,2,0:T(8,128)(2,1)S(1)}, bf16[2,576,576]{1,2,0:T(8,128)(2,1)}, u32[]{:S(2)}) copy-start(bf16[2,576,576]{1,2,0:T(8,128)(2,1)} %copy-done.3) | copy-start | bytes 3981316
  128.0 7.0 %copy-start.6 = (bf16[2,576,576]{1,2,0:T(8,128)(2,1)S(1)}, bf16[2,576,576]{1,2,0:T(8,128)(2,1)}, u32[]{:S(2)}) copy-start(bf16[2,576,576]{1,2,0:T(8,128)(2,1)} %copy-done.5) | copy-start | bytes 3981316
  128.0 20.3 %all-to-all-start.7 = ((f32[4,576,128]{2,1,0:T(8,128)}), f32[4,576,128]{2,1,0:T(8,128)}, u32[]{:S(2)}, u32[]{:S(2)}) async-start(f32[4,576,128]{2,1,0:T(8,128)} %fusion.34), calls=%async_computation.7 | async-start | bytes 2359296 | tf_op jit(solution)/shard_map/all_to_all | solution.py:110
  148.3 19.3 %all-to-all-start.5 = ((f32[4,576,128]{2,1,0:T(8,128)}), f32[4,576,128]{2,1,0:T(8,128)S(1)}, u32[]{:S(2)}, u32[]{:S(2)}) async-start(f32[4,576,128]{2,1,0:T(8,128)} %fusion.32), calls=%async_computation.5 | async-start | bytes 2359296 | tf_op jit(solution)/shard_map/all_to_all | solution.py:109
  167.7 13.4 %all-to-all-start.8 = ((bf16[8,2,4608]{2,1,0:T(2,128)(2,1)}), bf16[8,2,4608]{2,1,0:T(2,128)(2,1)S(1)}, u32[]{:S(2)}, u32[]{:S(2)}) async-start(bf16[8,2,4608]{2,1,0:T(2,128)(2,1)} %reshape.391), calls=%async_computation.8 | async-start | bytes 294912 | tf_op jit(solution)/shard_map/all_to_all | solution.py:120
  181.0 10.8 %all-to-all-start.6 = ((bf16[8,2,4608]{2,1,0:T(2,128)(2,1)}), bf16[8,2,4608]{2,1,0:T(2,128)(2,1)S(1)}, u32[]{:S(2)}, u32[]{:S(2)}) async-start(bf16[8,2,4608]{2,1,0:T(2,128)(2,1)} %reshape.389), calls=%async_computation.6 | async-start | bytes 294912 | tf_op jit(solution)/shard_map/all_to_all | solution.py:119
  (5 other events, 10.0 us)
where the time goes:
time: 194 us; the launch traced here: 193 us
  starting transfers between devices  46.5 us (24%)
  local copies, waits for them, and re-layouts  38.9 us (20%)
  other arithmetic  34.3 us (18%)
  waiting for transfers between devices  31 us (16%)
  matrix products  21.4 us (11%)
  blocking collectives  15.2 us (8%)
  between operations  5.28 us (3%)
    unnamed x68, local copies, waits for them, and re-layouts  17.3 us
    unnamed x7, other arithmetic  14.1 us
    all_to_all x1, waiting for transfers between devices, local(): lax.all_to_all(results[1], 'frame', split_axis=0, concat_axis=0, tiled=True)  11.9 us
    all_gather x1, blocking collectives, local(): lax.all_gather(v_wide, 'frame', axis=0, tiled=True)  7.64 us
    all_gather x1, blocking collectives, local(): lax.all_gather(k_wide, 'frame', axis=0, tiled=True)  7.53 us
    all_to_all x1, starting transfers between devices, local(): lax.all_to_all(keys_in, 'within', split_axis=2, concat_axis=1, tiled=True)  7.31 us
    convert_element_type x1, other arithmetic, grads(): dscore_low = dscore.astype(jnp.bfloat16)  7 us
    another operation x6, local copies, waits for them, and re-layouts  6.93 us
  transfers between devices with their start and end apart: 9, of which 5 were waited for; matrix products, arithmetic and copies ran while one was open for 26% of the time, Pallas kernels for 0%

commit v1 on v0

--- a/solution.py
+++ b/solution.py
@@ -11,7 +11,12 @@
         lax.all_to_all(queries, "within", split_axis=2, concat_axis=1, tiled=True),
         lax.all_to_all(keys_in, "within", split_axis=2, concat_axis=1, tiled=True),
         lax.all_to_all(values_in, "within", split_axis=2, concat_axis=1, tiled=True),
-        lax.all_to_all(grad_out, "within", split_axis=2, concat_axis=1, tiled=True),
+        jnp.concatenate(
+            lax.all_to_all(
+                jnp.stack(jnp.split(grad_out, lax.axis_size("within"), axis=2)), "within", 0, 0
+            ),
+            axis=1,
+        ),
     )
     seq = q_wide.shape[1]
     cols = q_wide.shape[2]

time: 194 us -> 200 us (1.031)
  local copies, waits for them, and re-layouts: 38.9 us -> 46.6 us
  other arithmetic: 34.3 us -> 32.3 us
    unnamed x68 -> x67, local copies, waits for them, and re-layouts: 17.3 us -> 24.1 us
    unnamed x7 -> x6, other arithmetic: 14.1 us -> 11.8 us
    another operation x6 -> x7, local copies, waits for them, and re-layouts: 6.93 us -> 8.27 us
  transfers between devices with their start and end apart: 9 -> 9, of which waited for: 5 -> 6; matrix products, arithmetic and copies ran while one was open for 26% -> 29% of each run, Pallas kernels for 0% -> 0%
where the time goes in v1:
time: 200 us; the launch traced here: 198 us
  local copies, waits for them, and re-layouts  46.6 us (23%)
  starting transfers between devices  45.6 us (23%)
  other arithmetic  32.3 us (16%)
  waiting for transfers between devices  32 us (16%)
  matrix products  21.3 us (11%)
  blocking collectives  15.2 us (8%)
  between operations  4.82 us (2%)
    unnamed x67, local copies, waits for them, and re-layouts  24.1 us
    all_to_all x1, waiting for transfers between devices, local(): lax.all_to_all(results[1], 'frame', split_axis=0, concat_axis=0, tiled=True)  11.9 us
    unnamed x6, other arithmetic  11.8 us
    all_gather x1, blocking collectives, local(): lax.all_gather(v_wide, 'frame', axis=0, tiled=True)  7.64 us
    all_gather x1, blocking collectives, local(): lax.all_gather(k_wide, 'frame', axis=0, tiled=True)  7.53 us
    all_to_all x1, starting transfers between devices, local(): lax.all_to_all(keys_in, 'within', split_axis=2, concat_axis=1, tiled=True)  7.31 us
    convert_element_type x1, other arithmetic, grads(): dscore_low = dscore.astype(jnp.bfloat16)  7 us
    another operation x6, local copies, waits for them, and re-layouts  6.93 us
  transfers between devices with their start and end apart: 9, of which 6 were waited for; matrix products, arithmetic and copies ran while one was open for 29% of the time, Pallas kernels for 0%

profile of v1, /device:TPU:0, one launch (start us, length us, event | category | flops | bytes accessed | tf_op | source)
XLA Modules:
  0.0 197.8 jit_solution(6116029653867502488)
XLA Ops:
  2.5 2.4 %reduce.31 = bf16[1024,72]{1,0:T(8,128)(2,1)S(1)} reduce(bf16[1024,1,72]{2,1,0:T(2,128)(2,1)S(1)} %bitcast.202, bf16[]{:T(256)} %broadcast.254), dimensions={1}, to_apply=%bitcast.157.reduce_sub_computation | reduce | bytes 294914
  6.0 7.3 %all-to-all-start.1 = ((bf16[8,2,4608]{2,1,0:T(2,128)(2,1)}), bf16[8,2,4608]{2,1,0:T(2,128)(2,1)S(1)}, u32[]{:S(2)}, u32[]{:S(2)}) async-start(bf16[8,2,4608]{2,1,0:T(2,128)(2,1)} %reshape.379), calls=%async_computation.1 | async-start | bytes 294912 | tf_op jit(solution)/shard_map/all_to_all | solution.py:12
  29.6 2.4 %reduce.30 = bf16[1024,72]{1,0:T(8,128)(2,1)S(1)} reduce(bf16[1024,1,72]{2,1,0:T(2,128)(2,1)S(1)} %bitcast.206, bf16[]{:T(256)} %broadcast.254), dimensions={1}, to_apply=%bitcast.159.reduce_sub_computation | reduce | bytes 294914
  35.1 6.0 %all-to-all-start.3 = ((bf16[8,2,4608]{2,1,0:T(2,128)(2,1)}), bf16[8,2,4608]{2,1,0:T(2,128)(2,1)S(1)}, u32[]{:S(2)}, u32[]{:S(2)}) async-start(bf16[8,2,4608]{2,1,0:T(2,128)(2,1)} %reshape.381), calls=%async_computation.3 | async-start | bytes 294912 | tf_op jit(solution)/shard_map/all_to_all | solution.py:13
  42.8 2.4 %reduce.32 = bf16[1024,72]{1,0:T(8,128)(2,1)S(1)} reduce(bf16[1024,1,72]{2,1,0:T(2,128)(2,1)S(1)} %bitcast.207, bf16[]{:T(256)} %broadcast.254), dimensions={1}, to_apply=%bitcast.161.reduce_sub_computation | reduce | bytes 294914
  48.6 5.1 %all-to-all-start = ((bf16[8,2,4608]{2,1,0:T(2,128)(2,1)}), bf16[8,2,4608]{2,1,0:T(2,128)(2,1)S(1)}, u32[]{:S(2)}, u32[]{:S(2)}) async-start(bf16[8,2,4608]{2,1,0:T(2,128)(2,1)} %reshape.383), calls=%async_computation | async-start | bytes 294912 | tf_op jit(solution)/shard_map/all_to_all | solution.py:11
  55.0 7.5 %all_gather.6 = bf16[4,576,128]{2,1,0:T(8,128)(2,1)S(1)} all-gather(bf16[1,576,128]{2,1,0:T(8,128)(2,1)S(1)} %bitcast.232), channel_id=1, replica_groups=mesh['frame'=4,'within'=8] {'frame'}, dimensions={0}, use_global_device_ids=true | all-gather | bytes 737280 | tf_op jit(solution)/shard_map/all_gather | solution.py:89
  62.5 7.6 %all_gather.7 = bf16[4,576,128]{2,1,0:T(8,128)(2,1)S(1)} all-gather(bf16[1,576,128]{2,1,0:T(8,128)(2,1)S(1)} %bitcast.236), channel_id=1, replica_groups=mesh['frame'=4,'within'=8] {'frame'}, dimensions={0}, use_global_device_ids=true | all-gather | bytes 737280 | tf_op jit(solution)/shard_map/all_gather | solution.py:90
  70.2 6.0 %all-to-all-start.2 = ((bf16[8,1,72,128]{3,2,1,0:T(8,128)(2,1)}), bf16[8,1,72,128]{3,2,1,0:T(8,128)(2,1)S(1)}, u32[]{:S(2)}, u32[]{:S(2)}) async-start(bf16[8,1,72,128]{3,2,1,0:T(8,128)(2,1)} %constant_dynamic-update-slice_fusion), calls=%async_computation.2 | async-start | bytes 294912 | tf_op jit(solution)/shard_map/all_to_all | solution.py:15
  80.0 3.9 %all-to-all-done.2 = bf16[8,1,72,128]{3,2,1,0:T(8,128)(2,1)S(1)} async-done(((bf16[8,1,72,128]{3,2,1,0:T(8,128)(2,1)}), bf16[8,1,72,128]{3,2,1,0:T(8,128)(2,1)S(1)}, u32[]{:S(2)}, u32[]{:S(2)}) %all-to-all-start.2) | async-done | bytes 147488 | tf_op jit(solution)/shard_map/all_to_all | solution.py:15
  90.8 2.7 %fusion.8 = (f32[2,576]{1,0:T(2,128)S(1)}, f32[2,576]{1,0:T(2,128)S(1)}, f32[2,576,576]{1,2,0:T(8,128)}) fusion(f32[2,576,576]{2,1,0:T(8,128)S(1)} %get-tuple-element.99, f32[2,576]{1,0:T(2,128)S(1)} %get-tuple-element.98, pred[576]{0:T(1024)(128)(4,1)S(1)} %get-tuple-element.109, bf16[576,2,64]{0,2,1:T(8,128)(2,1)S(1)} %copy.155, ...), kind=kOutput, calls=%fused_computation.24 | convolution fusion | flops 88913664 | bytes 5617728 | tf_op jit(solution)/shard_map/qhd,khd->hqk/dot_general | solution.py:54
  93.6 2.7 %fusion.7 = (f32[2,576]{1,0:T(2,128)S(1)}, f32[2,576]{1,0:T(2,128)S(1)}, f32[2,576,576]{1,2,0:T(8,128)}) fusion(f32[2,576,576]{2,1,0:T(8,128)S(1)} %get-tuple-element.102, f32[2,576]{1,0:T(2,128)S(1)} %get-tuple-element.101, pred[576]{0:T(1024)(128)(4,1)S(1)} %get-tuple-element.110, bf16[576,2,64]{0,2,1:T(8,128)(2,1)S(1)} %copy.155, ...), kind=kOutput, calls=%fused_computation.23 | convolution fusion | flops 88913664 | bytes 5617728 | tf_op jit(solution)/shard_map/qhd,khd->hqk/dot_general | solution.py:54
  96.3 2.5 %fusion.6 = (f32[2,576]{1,0:T(2,128)S(1)}, f32[2,576]{1,0:T(2,128)S(1)}, f32[2,576,576]{1,2,0:T(8,128)}) fusion(f32[2,576,576]{1,2,0:T(8,128)S(1)} %get-tuple-element.105, f32[2,576]{1,0:T(2,128)S(1)} %get-tuple-element.104, bf16[576,2,64]{0,2,1:T(8,128)(2,1)S(1)} %copy.155, bf16[576,2,64]{0,2,1:T(8,128)(2,1)S(1)} %copy-done.14), kind=kOutput, calls=%fused_computation.22 | convolution fusion | flops 88250112 | bytes 5617152 | tf_op jit(solution)/shard_map/qhd,khd->hqk/dot_general | solution.py:70
  109.8 7.0 %multiply_convert_fusion.1 = (bf16[2,576,576]{1,2,0:T(8,128)(2,1)S(1)}, bf16[2,576,576]{1,2,0:T(8,128)(2,1)S(1)}, bf16[2,576,576]{1,2,0:T(8,128)(2,1)S(1)}) fusion(f32[2,576,576]{1,2,0:T(8,128)} %get-tuple-element.103, f32[2,576]{1,0:T(2,128)S(1)} %get-tuple-element.88, f32[2,576]{1,0:T(2,128)S(1)} %get-tuple-element.87, f32[2,576]{1,0:T(2,128)S(1)} %get-tuple-element.92, ...), kind=kLoop, calls=%fused_computation.13 | loop fusion | flops 13271040 | bytes 19921536 | tf_op jit(solution)/shard_map/convert_element_type | solution.py:72
  121.4 4.0 %all-to-all-start.4 = ((bf16[8,2,4608]{2,1,0:T(2,128)(2,1)}), bf16[8,2,4608]{2,1,0:T(2,128)(2,1)}, u32[]{:S(2)}, u32[]{:S(2)}) async-start(bf16[8,2,4608]{2,1,0:T(2,128)(2,1)} %reshape.385), calls=%async_computation.4 | async-start | bytes 294912 | tf_op jit(solution)/shard_map/all_to_all | solution.py:123
  127.2 2.5 %fusion.27 = f32[4,576,128]{2,1,0:T(8,128)} fusion(f32[4,576,128]{2,1,0:T(8,128)} %constant_dynamic-update-slice_fusion.8, s32[]{:T(128)} %select_n.49, f32[1,576,128]{2,1,0:T(8,128)} %copy.140, pred[]{:T(512)} %get-tuple-element.82), kind=kLoop, calls=%fused_computation.52 | loop fusion | flops 147456 | bytes 885760 | tf_op jit(solution)/shard_map/scatter-add | solution.py:110
  133.2 4.4 %all-to-all-start.7 = ((f32[4,576,128]{2,1,0:T(8,128)}), f32[4,576,128]{2,1,0:T(8,128)}, u32[]{:S(2)}, u32[]{:S(2)}) async-start(f32[4,576,128]{2,1,0:T(8,128)} %fusion.28), calls=%async_computation.7 | async-start | bytes 2359296 | tf_op jit(solution)/shard_map/all_to_all | solution.py:115
  147.3 6.2 %all-to-all-done.7 = f32[4,576,128]{2,1,0:T(8,128)} async-done(((f32[4,576,128]{2,1,0:T(8,128)}), f32[4,576,128]{2,1,0:T(8,128)}, u32[]{:S(2)}, u32[]{:S(2)}) %all-to-all-start.7) | async-done | bytes 1179680 | tf_op jit(solution)/shard_map/all_to_all | solution.py:115
  153.5 3.5 %all-to-all-start.5 = ((f32[4,576,128]{2,1,0:T(8,128)}), f32[4,576,128]{2,1,0:T(8,128)S(1)}, u32[]{:S(2)}, u32[]{:S(2)}) async-start(f32[4,576,128]{2,1,0:T(8,128)} %fusion.26), calls=%async_computation.5 | async-start | bytes 2359296 | tf_op jit(solution)/shard_map/all_to_all | solution.py:114
  161.0 11.9 %all-to-all-done.5 = f32[4,576,128]{2,1,0:T(8,128)S(1)} async-done(((f32[4,576,128]{2,1,0:T(8,128)}), f32[4,576,128]{2,1,0:T(8,128)S(1)}, u32[]{:S(2)}, u32[]{:S(2)}) %all-to-all-start.5) | async-done | bytes 1179680 | tf_op jit(solution)/shard_map/all_to_all | solution.py:114
  172.8 5.9 %all-to-all-start.8 = ((bf16[8,2,4608]{2,1,0:T(2,128)(2,1)}), bf16[8,2,4608]{2,1,0:T(2,128)(2,1)S(1)}, u32[]{:S(2)}, u32[]{:S(2)}) async-start(bf16[8,2,4608]{2,1,0:T(2,128)(2,1)} %reshape.389), calls=%async_computation.8 | async-start | bytes 294912 | tf_op jit(solution)/shard_map/all_to_all | solution.py:125
  181.4 4.8 %all-to-all-done.8 = bf16[8,2,4608]{2,1,0:T(2,128)(2,1)S(1)} async-done(((bf16[8,2,4608]{2,1,0:T(2,128)(2,1)}), bf16[8,2,4608]{2,1,0:T(2,128)(2,1)S(1)}, u32[]{:S(2)}, u32[]{:S(2)}) %all-to-all-start.8) | async-done | bytes 147488 | tf_op jit(solution)/shard_map/all_to_all | solution.py:125
  186.2 3.4 %all-to-all-start.6 = ((bf16[8,2,4608]{2,1,0:T(2,128)(2,1)}), bf16[8,2,4608]{2,1,0:T(2,128)(2,1)S(1)}, u32[]{:S(2)}, u32[]{:S(2)}) async-start(bf16[8,2,4608]{2,1,0:T(2,128)(2,1)} %reshape.387), calls=%async_computation.6 | async-start | bytes 294912 | tf_op jit(solution)/shard_map/all_to_all | solution.py:124
  192.6 4.4 %all-to-all-done.6 = bf16[8,2,4608]{2,1,0:T(2,128)(2,1)S(1)} async-done(((bf16[8,2,4608]{2,1,0:T(2,128)(2,1)}), bf16[8,2,4608]{2,1,0:T(2,128)(2,1)S(1)}, u32[]{:S(2)}, u32[]{:S(2)}) %all-to-all-start.6) | async-done | bytes 147488 | tf_op jit(solution)/shard_map/all_to_all | solution.py:124
  (135 shorter events, 76.5 us)
Async XLA Ops:
  0.6 12.7 %copy-start = (s32[4,2]{0,1:T(2,128)S(1)}, s32[4,2]{0,1:T(2,128)}, u32[]{:S(2)}) copy-start(s32[4,2]{0,1:T(2,128)} %param.22) | copy-start | bytes 100
  0.6 32.5 %copy-start.17 = (s32[4]{0:T(128)S(1)}, s32[4]{0:T(128)}, u32[]{:S(2)}) copy-start(s32[4]{0:T(128)} %param.23) | copy-start | bytes 52
  0.7 41.7 %copy-start.16 = (bf16[1,72,1024]{2,1,0:T(8,128)(2,1)S(1)}, bf16[1,72,1024]{2,1,0:T(8,128)(2,1)}, u32[]{:S(2)}) copy-start(bf16[1,72,1024]{2,1,0:T(8,128)(2,1)} %param.18) | copy-start | bytes 442372
  6.0 29.1 %all-to-all-start.1 = ((bf16[8,2,4608]{2,1,0:T(2,128)(2,1)}), bf16[8,2,4608]{2,1,0:T(2,128)(2,1)S(1)}, u32[]{:S(2)}, u32[]{:S(2)}) async-start(bf16[8,2,4608]{2,1,0:T(2,128)(2,1)} %reshape.379), calls=%async_computation.1 | async-start | bytes 294912 | tf_op jit(solution)/shard_map/all_to_all | solution.py:12
  35.1 13.4 %all-to-all-start.3 = ((bf16[8,2,4608]{2,1,0:T(2,128)(2,1)}), bf16[8,2,4608]{2,1,0:T(2,128)(2,1)S(1)}, u32[]{:S(2)}, u32[]{:S(2)}) async-start(bf16[8,2,4608]{2,1,0:T(2,128)(2,1)} %reshape.381), calls=%async_computation.3 | async-start | bytes 294912 | tf_op jit(solution)/shard_map/all_to_all | solution.py:13
  48.6 21.6 %all-to-all-start = ((bf16[8,2,4608]{2,1,0:T(2,128)(2,1)}), bf16[8,2,4608]{2,1,0:T(2,128)(2,1)S(1)}, u32[]{:S(2)}, u32[]{:S(2)}) async-start(bf16[8,2,4608]{2,1,0:T(2,128)(2,1)} %reshape.383), calls=%async_computation | async-start | bytes 294912 | tf_op jit(solution)/shard_map/all_to_all | solution.py:11
  70.2 13.7 %all-to-all-start.2 = ((bf16[8,1,72,128]{3,2,1,0:T(8,128)(2,1)}), bf16[8,1,72,128]{3,2,1,0:T(8,128)(2,1)S(1)}, u32[]{:S(2)}, u32[]{:S(2)}) async-start(bf16[8,1,72,128]{3,2,1,0:T(8,128)(2,1)} %constant_dynamic-update-slice_fusion), calls=%async_computation.2 | async-start | bytes 294912 | tf_op jit(solution)/shard_map/all_to_all | solution.py:15
  88.5 2.3 %copy-start.13 = (bf16[1,576,128]{1,2,0:T(8,128)(2,1)S(1)}, bf16[1,576,128]{1,2,0:T(8,128)(2,1)}, u32[]{:S(2)}) copy-start(bf16[1,576,128]{1,2,0:T(8,128)(2,1)} %copy.122) | copy-start | bytes 442372
  90.1 8.7 %copy-start.1 = (f32[2,576,576]{2,1,0:T(8,128)}, f32[2,576,576]{2,1,0:T(8,128)S(1)}, u32[]{:S(2)}) copy-start(f32[2,576,576]{2,1,0:T(8,128)S(1)} %get-tuple-element.99) | copy-start | bytes 7962628
  90.8 9.7 %copy-start.2 = (f32[2,576,576]{2,1,0:T(8,128)}, f32[2,576,576]{2,1,0:T(8,128)S(1)}, u32[]{:S(2)}) copy-start(f32[2,576,576]{2,1,0:T(8,128)S(1)} %get-tuple-element.102) | copy-start | bytes 7962628
  90.8 2.7 %copy-start.15 = (bf16[1,576,128]{1,2,0:T(8,128)(2,1)S(1)}, bf16[1,576,128]{1,2,0:T(8,128)(2,1)}, u32[]{:S(2)}) copy-start(bf16[1,576,128]{1,2,0:T(8,128)(2,1)} %copy.121) | copy-start | bytes 442372
  93.6 2.7 %copy-start.14 = (bf16[576,2,64]{0,2,1:T(8,128)(2,1)S(1)}, bf16[576,2,64]{0,2,1:T(8,128)(2,1)}, u32[]{:S(2)}) copy-start(bf16[576,2,64]{0,2,1:T(8,128)(2,1)} %reshape_squeeze.29) | copy-start | bytes 442372
  109.8 7.0 %copy-start.10 = (bf16[576,2,64]{0,2,1:T(8,128)(2,1)S(1)}, bf16[576,2,64]{0,2,1:T(8,128)(2,1)}, u32[]{:S(2)}) copy-start(bf16[576,2,64]{0,2,1:T(8,128)(2,1)} %reshape_squeeze.26) | copy-start | bytes 442372
  109.8 7.4 %copy-start.9 = (bf16[1,576,128]{1,2,0:T(8,128)(2,1)S(1)}, bf16[1,576,128]{1,2,0:T(8,128)(2,1)}, u32[]{:S(2)}) copy-start(bf16[1,576,128]{1,2,0:T(8,128)(2,1)} %copy.115) | copy-start | bytes 442372
  117.6 8.8 %copy-start.11 = (f32[1,576,128]{2,1,0:T(8,128)S(1)}, f32[1,576,128]{2,1,0:T(8,128)}, u32[]{:S(2)}) copy-start(f32[1,576,128]{2,1,0:T(8,128)} %copy.138) | copy-start | bytes 884740
  118.8 10.9 %copy-start.12 = (f32[1,576,128]{2,1,0:T(8,128)S(1)}, f32[1,576,128]{2,1,0:T(8,128)}, u32[]{:S(2)}) copy-start(f32[1,576,128]{2,1,0:T(8,128)} %copy.142) | copy-start | bytes 884740
  118.8 13.2 %copy-start.8 = (bf16[2,576,576]{1,2,0:T(8,128)(2,1)S(1)}, bf16[2,576,576]{1,2,0:T(8,128)(2,1)}, u32[]{:S(2)}) copy-start(bf16[2,576,576]{1,2,0:T(8,128)(2,1)} %copy-done.7) | copy-start | bytes 3981316
  121.4 11.8 %all-to-all-start.4 = ((bf16[8,2,4608]{2,1,0:T(2,128)(2,1)}), bf16[8,2,4608]{2,1,0:T(2,128)(2,1)}, u32[]{:S(2)}, u32[]{:S(2)}) async-start(bf16[8,2,4608]{2,1,0:T(2,128)(2,1)} %reshape.385), calls=%async_computation.4 | async-start | bytes 294912 | tf_op jit(solution)/shard_map/all_to_all | solution.py:123
  127.2 10.4 %copy-start.4 = (bf16[2,576,576]{1,2,0:T(8,128)(2,1)S(1)}, bf16[2,576,576]{1,2,0:T(8,128)(2,1)}, u32[]{:S(2)}) copy-start(bf16[2,576,576]{1,2,0:T(8,128)(2,1)} %copy-done.3) | copy-start | bytes 3981316
  133.1 7.0 %copy-start.6 = (bf16[2,576,576]{1,2,0:T(8,128)(2,1)S(1)}, bf16[2,576,576]{1,2,0:T(8,128)(2,1)}, u32[]{:S(2)}) copy-start(bf16[2,576,576]{1,2,0:T(8,128)(2,1)} %copy-done.5) | copy-start | bytes 3981316
  133.2 20.3 %all-to-all-start.7 = ((f32[4,576,128]{2,1,0:T(8,128)}), f32[4,576,128]{2,1,0:T(8,128)}, u32[]{:S(2)}, u32[]{:S(2)}) async-start(f32[4,576,128]{2,1,0:T(8,128)} %fusion.28), calls=%async_computation.7 | async-start | bytes 2359296 | tf_op jit(solution)/shard_map/all_to_all | solution.py:115
  153.5 19.3 %all-to-all-start.5 = ((f32[4,576,128]{2,1,0:T(8,128)}), f32[4,576,128]{2,1,0:T(8,128)S(1)}, u32[]{:S(2)}, u32[]{:S(2)}) async-start(f32[4,576,128]{2,1,0:T(8,128)} %fusion.26), calls=%async_computation.5 | async-start | bytes 2359296 | tf_op jit(solution)/shard_map/all_to_all | solution.py:114
  172.8 13.4 %all-to-all-start.8 = ((bf16[8,2,4608]{2,1,0:T(2,128)(2,1)}), bf16[8,2,4608]{2,1,0:T(2,128)(2,1)S(1)}, u32[]{:S(2)}, u32[]{:S(2)}) async-start(bf16[8,2,4608]{2,1,0:T(2,128)(2,1)} %reshape.389), calls=%async_computation.8 | async-start | bytes 294912 | tf_op jit(solution)/shard_map/all_to_all | solution.py:125
  186.2 10.8 %all-to-all-start.6 = ((bf16[8,2,4608]{2,1,0:T(2,128)(2,1)}), bf16[8,2,4608]{2,1,0:T(2,128)(2,1)S(1)}, u32[]{:S(2)}, u32[]{:S(2)}) async-start(bf16[8,2,4608]{2,1,0:T(2,128)(2,1)} %reshape.387), calls=%async_computation.6 | async-start | bytes 294912 | tf_op jit(solution)/shard_map/all_to_all | solution.py:124
  (3 other events, 4.8 us)
